TPU v7x, 256 devices: a whole 4x4x8 slice. The times are simulated.
256 devices in a mesh: cfg: 2 (over core), blk: 4 (over y), uly: 32 (over x, z).
Axes of the slice: x: 4, y: 4, z: 8, core: 2. Of those that a mesh axis runs over, the one named last changes fastest.
Arguments:
- queries: bfloat16 [16384, 4096], P(('cfg', 'blk', 'uly')), parts along dimension 0, may hold values from -24 to 24
- key_states: bfloat16 [16384, 4096], P(('cfg', 'blk', 'uly')), parts along dimension 0, may hold values from -24 to 24
- value_states: bfloat16 [16384, 4096], P(('cfg', 'blk', 'uly')), parts along dimension 0, may hold values from -6 to 6
- tile_list: int32 [16, 12], replicated, may hold values from 0 to 15, as said below
- tile_used: int32 [16], replicated, may hold values from 1 to 12, as said below
Outputs:
- attended: bfloat16 [16384, 4096], P(('cfg', 'blk', 'uly')), parts along dimension 0
There are 2 independent parts, one for each index of `cfg`. A program takes and returns all parts, laid end to end along the dimension named above; an argument that names none is the same for every part. Nothing has to cross between parts.
Inputs may be any that keep to these rules, and one draw needn't show every extreme that they name: `tile_list`: tiles are numbered with the temporal tile row slowest, then 2 rows along the height, then 2 along the width. The first tile_used[i] entries of row i are distinct tiles whose temporal tile row differs from that of tile i by at most one, and the first of them is tile i itself; the other entries of the row are to be ignored. `tile_used`: in every draw some tile lists all 12 tiles of its window and some tile lists only itself.
All inputs are finite; a program needn't handle non-finite values.
Results may differ from a plain program's by a relative error of at most 0.0047.
Values may be sent and summed in bfloat16 or wider, within the bound.
No kernel may reach another device: no remote copies, remote signals or barrier semaphores. Data moves between devices by JAX's collectives and lax.ppermute only.
A program may use at most 64 MiB of HBM per device.

v0:
```python
import jax
import jax.numpy as jnp
from jax import lax
from jax.sharding import PartitionSpec as P

HD = 128
TILE = 512
TH = 2
TW = 2


MASKED_SCORE = -1e30


def padded(block, sides, width):
    for axis, dim in sides:
        count = lax.axis_size(axis)
        forward = [(i, i + 1) for i in range(count - 1)]
        backward = [(target, source) for source, target in forward]
        low = lax.ppermute(
            lax.slice_in_dim(block, block.shape[dim] - width, None, axis=dim), axis, forward
        )
        high = lax.ppermute(lax.slice_in_dim(block, 0, width, axis=dim), axis, backward)
        block = jnp.concatenate([low, block, high], axis=dim)
    return block


def attended_table(tile_list, tile_used):
    slot_ids = jnp.arange(tile_list.shape[1], dtype=jnp.int32)
    live = slot_ids[None, :] < tile_used[:, None]
    tile_ids = jnp.arange(tile_list.shape[0], dtype=jnp.int32)
    hits = (tile_list[:, :, None] == tile_ids[None, None, :]) & live[:, :, None]
    return jnp.any(hits, axis=1).astype(jnp.float32)


def allow_rows(local_rows, row_tiles):
    tile_ids = jnp.arange(local_rows.shape[1], dtype=jnp.int32)
    onehot = (tile_ids[:, None] == row_tiles[None, :]).astype(jnp.float32)
    return jnp.dot(local_rows, onehot, precision=lax.Precision.HIGHEST) > 0.5


def absorb(running, query_tile, key_piece, value_piece, allowed):
    row_max, row_total, weighted = running
    scores = jnp.einsum(
        "qhd,khd->hqk", query_tile, key_piece, preferred_element_type=jnp.float32
    ) * HD ** (-0.5)
    masked = jnp.where(allowed[None, None, :], scores, MASKED_SCORE)
    new_max = jnp.maximum(row_max, jnp.max(masked, axis=-1))
    weights = jnp.where(
        allowed[None, None, :], jnp.exp(scores - new_max[:, :, None]), jnp.float32(0.0)
    )
    row_total = jnp.sum(weights, axis=-1)
    update = jnp.einsum(
        "hqk,khd->qhd",
        weights.astype(jnp.bfloat16),
        value_piece,
        preferred_element_type=jnp.float32,
    )
    weighted = update
    return (new_max, row_total, weighted)


def finish(row_total, weighted):
    return (weighted / jnp.swapaxes(row_total, -1, -2)[..., None]).astype(jnp.bfloat16)


def body(queries, key_states, value_states, tile_list, tile_used):
    block_index = lax.axis_index("blk")
    tok_rows = queries.shape[0]
    slab_tiles = TH * TW
    slab_rows = slab_tiles * TILE
    stacked = jnp.stack([key_states, value_states])
    beside = padded(stacked, (("blk", 1),), tok_rows)
    key_lower = beside[0, :tok_rows]
    value_lower = beside[1, :tok_rows]
    key_upper = beside[0, 2 * tok_rows :]
    value_upper = beside[1, 2 * tok_rows :]
    moved = (
        lax.all_to_all(queries, "uly", split_axis=1, concat_axis=0, tiled=True),
        lax.all_to_all(key_states, "uly", split_axis=1, concat_axis=0, tiled=True),
        lax.all_to_all(value_states, "uly", split_axis=1, concat_axis=0, tiled=True),
        lax.all_to_all(key_lower, "uly", split_axis=1, concat_axis=0, tiled=True),
        lax.all_to_all(value_lower, "uly", split_axis=1, concat_axis=0, tiled=True),
        lax.all_to_all(key_upper, "uly", split_axis=1, concat_axis=0, tiled=True),
        lax.all_to_all(value_upper, "uly", split_axis=1, concat_axis=0, tiled=True),
    )
    (
        query_block,
        key_block,
        value_block,
        key_low_block,
        value_low_block,
        key_up_block,
        value_up_block,
    ) = moved
    block_rows, row_width = query_block.shape
    key_full = jnp.concatenate([key_low_block, key_block, key_up_block], axis=0)
    value_full = jnp.concatenate([value_low_block, value_block, value_up_block], axis=0)
    extended = jnp.stack([key_full, value_full])
    heads_here = row_width // HD
    tiles_here = block_rows // TILE
    slabs_here = tiles_here // slab_tiles
    allowed_tiles = attended_table(tile_list, tile_used)
    local_rows = lax.dynamic_slice_in_dim(allowed_tiles, block_index * tiles_here, tiles_here, 0)
    query_tiles = query_block.reshape(tiles_here, TILE, heads_here, HD)
    extended = extended.reshape(2, block_rows + 2 * slab_rows, heads_here, HD)

    def one_tile(packed):
        tile_index, query_tile = packed
        slab_index = tile_index // slab_tiles
        key_window = extended[0]
        value_window = extended[1]
        global_slab = block_index * slabs_here + slab_index
        row_tiles = (global_slab - 1) * slab_tiles + jnp.arange(
            3 * slab_rows, dtype=jnp.int32
        ) // TILE
        tile_row = lax.dynamic_slice_in_dim(local_rows, tile_index, 1, 0)
        allowed = allow_rows(tile_row, row_tiles)[0]
        initial = (
            jnp.full((heads_here, TILE), MASKED_SCORE, jnp.float32),
            jnp.zeros((heads_here, TILE), jnp.float32),
            jnp.zeros((TILE, heads_here, HD), jnp.float32),
        )
        new_max, row_total, weighted = absorb(
            initial, query_tile, key_window, value_window, allowed
        )
        return finish(row_total, weighted)

    result = lax.map(one_tile, (jnp.arange(tiles_here, dtype=jnp.int32), query_tiles))
    attended_block = result.reshape(block_rows, row_width)
    return lax.all_to_all(attended_block, "uly", split_axis=0, concat_axis=1, tiled=True)


def solution(mesh):
    in_specs = (
        P(("cfg", "blk", "uly"), None),
        P(("cfg", "blk", "uly"), None),
        P(("cfg", "blk", "uly"), None),
        P(),
        P(),
    )
    out_specs = P(("cfg", "blk", "uly"), None)
    return jax.shard_map(body, mesh=mesh, in_specs=in_specs, out_specs=out_specs, check_vma=False)
```

profile of v0, /device:TPU:48, one launch (start us, length us, event | category | flops | bytes accessed | tf_op | source)
XLA Modules:
  0.0 229.7 jit_solution(12545796300731043732)
XLA Ops:
  0.0 2.1 copy_bitcast_fusion.2
  2.1 11.2 %all-to-all-start.2 = ((bf16[64,32,128]{2,0,1:T(8,128)(2,1)}), bf16[64,32,128]{2,0,1:T(8,128)(2,1)S(1)}, u32[]{:S(2)}, u32[]{:S(2)}) async-start(bf16[64,32,128]{2,0,1:T(8,128)(2,1)} %copy_bitcast_fusion.2), calls=%async_computation.2 | async-start | bytes 1048576 | tf_op jit(solution)/shard_map/all_to_all | solution.py:80
  13.3 2.3 pad_maximum_fusion
  15.6 3.2 %collective-permute-start = (bf16[2,64,4096]{2,1,0:T(8,128)(2,1)}, bf16[2,64,4096]{2,1,0:T(8,128)(2,1)}, u32[]{:S(2)}, u32[]{:S(2)}) collective-permute-start(bf16[2,64,4096]{2,1,0:T(8,128)(2,1)} %pad_maximum_fusion), channel_id=1, source_target_pairs={{0,32},{32,64},{64,96},{1,33},{33,65},{65,97},{2,34},{34,66},{66,9... | collective-permute-start | bytes 3145736 | tf_op jit(solution)/shard_map/ppermute | solution.py:20
  18.8 0.9 copy_bitcast_fusion.1
  19.7 11.2 %all-to-all-done.2 = bf16[64,32,128]{2,0,1:T(8,128)(2,1)S(1)} async-done(((bf16[64,32,128]{2,0,1:T(8,128)(2,1)}), bf16[64,32,128]{2,0,1:T(8,128)(2,1)S(1)}, u32[]{:S(2)}, u32[]{:S(2)}) %all-to-all-start.2) | async-done | bytes 524320 | tf_op jit(solution)/shard_map/all_to_all | solution.py:80
  30.9 4.9 %all-to-all-start.5 = ((bf16[64,32,128]{2,0,1:T(8,128)(2,1)}), bf16[64,32,128]{2,0,1:T(8,128)(2,1)S(1)}, u32[]{:S(2)}, u32[]{:S(2)}) async-start(bf16[64,32,128]{2,0,1:T(8,128)(2,1)} %copy_bitcast_fusion.1), calls=%async_computation.5 | async-start | bytes 1048576 | tf_op jit(solution)/shard_map/all_to_all | solution.py:81
  35.8 2.4 %collective-permute-start.1 = (bf16[2,64,4096]{2,1,0:T(8,128)(2,1)}, bf16[2,64,4096]{2,1,0:T(8,128)(2,1)}, u32[]{:S(2)}, u32[]{:S(2)}) collective-permute-start(bf16[2,64,4096]{2,1,0:T(8,128)(2,1)} %pad_maximum_fusion), channel_id=1, source_target_pairs={{32,0},{64,32},{96,64},{33,1},{65,33},{97,65},{34,2},{66,34},{98,6... | collective-permute-start | bytes 3145736 | tf_op jit(solution)/shard_map/ppermute | solution.py:23
  38.1 4.0 %collective-permute-done = bf16[2,64,4096]{2,1,0:T(8,128)(2,1)} collective-permute-done((bf16[2,64,4096]{2,1,0:T(8,128)(2,1)}, bf16[2,64,4096]{2,1,0:T(8,128)(2,1)}, u32[]{:S(2)}, u32[]{:S(2)}) %collective-permute-start) | collective-permute-done | bytes 1048608 | tf_op jit(solution)/shard_map/ppermute | solution.py:20
  42.1 1.3 slice_bitcast_fusion.3
  43.4 0.1 copy.67
  43.5 1.0 copy.54
  44.5 8.2 %all-to-all-done.5 = bf16[64,32,128]{2,0,1:T(8,128)(2,1)S(1)} async-done(((bf16[64,32,128]{2,0,1:T(8,128)(2,1)}), bf16[64,32,128]{2,0,1:T(8,128)(2,1)S(1)}, u32[]{:S(2)}, u32[]{:S(2)}) %all-to-all-start.5) | async-done | bytes 524320 | tf_op jit(solution)/shard_map/all_to_all | solution.py:81
  52.7 4.9 %all-to-all-start.1 = ((bf16[64,32,128]{2,0,1:T(8,128)(2,1)}), bf16[64,32,128]{2,0,1:T(8,128)(2,1)S(1)}, u32[]{:S(2)}, u32[]{:S(2)}) async-start(bf16[64,32,128]{2,0,1:T(8,128)(2,1)} %copy.54), calls=%async_computation.1 | async-start | bytes 1048576 | tf_op jit(solution)/shard_map/all_to_all | solution.py:82
  57.6 4.1 %collective-permute-done.1 = bf16[2,64,4096]{2,1,0:T(8,128)(2,1)} collective-permute-done((bf16[2,64,4096]{2,1,0:T(8,128)(2,1)}, bf16[2,64,4096]{2,1,0:T(8,128)(2,1)}, u32[]{:S(2)}, u32[]{:S(2)}) %collective-permute-start.1) | collective-permute-done | bytes 1048608 | tf_op jit(solution)/shard_map/ppermute | solution.py:23
  61.6 2.1 slice_bitcast_fusion.2
  63.7 0.1 copy.68
  63.8 1.0 copy.56
  64.8 9.5 %all-to-all-done.1 = bf16[64,32,128]{2,0,1:T(8,128)(2,1)S(1)} async-done(((bf16[64,32,128]{2,0,1:T(8,128)(2,1)}), bf16[64,32,128]{2,0,1:T(8,128)(2,1)S(1)}, u32[]{:S(2)}, u32[]{:S(2)}) %all-to-all-start.1) | async-done | bytes 524320 | tf_op jit(solution)/shard_map/all_to_all | solution.py:82
  74.4 4.9 %all-to-all-start.3 = ((bf16[64,32,128]{2,0,1:T(8,128)(2,1)}), bf16[64,32,128]{2,0,1:T(8,128)(2,1)S(1)}, u32[]{:S(2)}, u32[]{:S(2)}) async-start(bf16[64,32,128]{2,0,1:T(8,128)(2,1)} %copy.56), calls=%async_computation.3 | async-start | bytes 1048576 | tf_op jit(solution)/shard_map/all_to_all | solution.py:84
  79.2 0.1 copy.69
  79.3 1.0 copy.57
  80.4 15.5 %all-to-all-done.3 = bf16[64,32,128]{2,0,1:T(8,128)(2,1)S(1)} async-done(((bf16[64,32,128]{2,0,1:T(8,128)(2,1)}), bf16[64,32,128]{2,0,1:T(8,128)(2,1)S(1)}, u32[]{:S(2)}, u32[]{:S(2)}) %all-to-all-start.3) | async-done | bytes 524320 | tf_op jit(solution)/shard_map/all_to_all | solution.py:84
  95.9 4.8 %all-to-all-start.4 = ((bf16[64,32,128]{2,0,1:T(8,128)(2,1)}), bf16[64,32,128]{2,0,1:T(8,128)(2,1)S(1)}, u32[]{:S(2)}, u32[]{:S(2)}) async-start(bf16[64,32,128]{2,0,1:T(8,128)(2,1)} %copy.57), calls=%async_computation.4 | async-start | bytes 1048576 | tf_op jit(solution)/shard_map/all_to_all | solution.py:83
  100.7 0.0 copy-done.7
  100.8 0.1 copy.52
  100.9 0.1 fusion.49
  101.0 1.1 copy.70
  102.1 1.0 copy.59
  103.1 13.6 %all-to-all-done.4 = bf16[64,32,128]{2,0,1:T(8,128)(2,1)S(1)} async-done(((bf16[64,32,128]{2,0,1:T(8,128)(2,1)}), bf16[64,32,128]{2,0,1:T(8,128)(2,1)S(1)}, u32[]{:S(2)}, u32[]{:S(2)}) %all-to-all-start.4) | async-done | bytes 524320 | tf_op jit(solution)/shard_map/all_to_all | solution.py:83
  116.7 4.9 %all-to-all-start.6 = ((bf16[64,32,128]{2,0,1:T(8,128)(2,1)}), bf16[64,32,128]{2,0,1:T(8,128)(2,1)}, u32[]{:S(2)}, u32[]{:S(2)}) async-start(bf16[64,32,128]{2,0,1:T(8,128)(2,1)} %copy.59), calls=%async_computation.6 | async-start | bytes 1048576 | tf_op jit(solution)/shard_map/all_to_all | solution.py:85
  121.7 0.9 copy_bitcast_fusion.3
  122.6 0.0 copy-done.3
  122.6 0.0 copy-done.5
  122.6 1.3 maximum_bitcast_fusion.1
  124.0 13.0 %all-to-all-done.6 = bf16[64,32,128]{2,0,1:T(8,128)(2,1)} async-done(((bf16[64,32,128]{2,0,1:T(8,128)(2,1)}), bf16[64,32,128]{2,0,1:T(8,128)(2,1)}, u32[]{:S(2)}, u32[]{:S(2)}) %all-to-all-start.6) | async-done | bytes 524320 | tf_op jit(solution)/shard_map/all_to_all | solution.py:85
  137.0 4.9 %all-to-all-start = ((bf16[64,32,128]{2,0,1:T(8,128)(2,1)}), bf16[64,32,128]{2,0,1:T(8,128)(2,1)S(1)}, u32[]{:S(2)}, u32[]{:S(2)}) async-start(bf16[64,32,128]{2,0,1:T(8,128)(2,1)} %copy_bitcast_fusion.3), calls=%async_computation | async-start | bytes 1048576 | tf_op jit(solution)/shard_map/all_to_all | solution.py:79
  141.9 1.3 maximum_bitcast_fusion.2
  143.2 0.0 copy-start.6
  143.2 1.9 maximum_bitcast_fusion
  145.1 11.6 %all-to-all-done = bf16[64,32,128]{2,0,1:T(8,128)(2,1)S(1)} async-done(((bf16[64,32,128]{2,0,1:T(8,128)(2,1)}), bf16[64,32,128]{2,0,1:T(8,128)(2,1)S(1)}, u32[]{:S(2)}, u32[]{:S(2)}) %all-to-all-start) | async-done | bytes 524320 | tf_op jit(solution)/shard_map/all_to_all | solution.py:79
  156.7 53.5 %while.13 = (s32[]{:T(128)}, bf16[4,512,1,128]{3,1,2,0:T(8,128)(2,1)S(1)}, s32[4]{0:T(128)S(1)}, f32[4,16]{1,0:T(4,128)S(1)}, s32[]{:T(128)}, /*index=5*/bf16[4,...) while((s32[]{:T(128)}, ...), condition=%wide.region_4.5_spmd, body=%wide.region_1.4_spmd.sunk | while | flops 1646685696 | bytes 53878148 | solution.py:129
  156.7 0.6 dynamic_slice.44
  161.2 0.2 fusion.65
  161.4 3.5 %select_reduce_fusion.2 = (f32[512]{0:T(512)S(1)}, f32[512,6144]{1,0:T(8,128)S(1)}) fusion(pred[6144]{0:T(1024)(128)(4,1)S(1)} %broadcast_compare_fusion.2, bf16[2,6144,1,128]{3,1,2,0:T(8,128)(2,1)} %get-tuple-element.256, bf16[4,512,1,128]{3,1,2,0:T(8,128)(2,1)S(1)} %get-tuple-element.255, s32[]{:T(128)} %get-tuple-element.237), kind=kOutput, calls=%fused_computation.1.clone.1 | convolution fusion | flops 814743040 | bytes 14295552 | tf_op jit(solution)/shard_map/while/body/eval_jaxpr/qhd,khd->hqk/dot_general | solution.py:44
  165.0 2.9 %fusion.66 = f32[512]{0:T(512)S(1)} fusion(f32[512,6144]{1,0:T(8,128)S(1)} %get-tuple-element.222, f32[512]{0:T(512)S(1)} %broadcast_maximum_fusion.2, pred[6144]{0:T(1024)(128)(4,1)S(1)} %broadcast_compare_fusion.2), kind=kLoop, calls=%fused_computation.2.clone.1 | loop fusion | flops 12582400 | bytes 12593152 | tf_op jit(solution)/shard_map/while/body/eval_jaxpr/reduce_sum | solution.py:52
  167.9 2.2 fusion.67
  170.0 0.6 dynamic_slice.44
  174.6 0.2 fusion.65
  174.8 3.5 %select_reduce_fusion.2 = (f32[512]{0:T(512)S(1)}, f32[512,6144]{1,0:T(8,128)S(1)}) fusion(pred[6144]{0:T(1024)(128)(4,1)S(1)} %broadcast_compare_fusion.2, bf16[2,6144,1,128]{3,1,2,0:T(8,128)(2,1)} %get-tuple-element.256, bf16[4,512,1,128]{3,1,2,0:T(8,128)(2,1)S(1)} %get-tuple-element.255, s32[]{:T(128)} %get-tuple-element.237), kind=kOutput, calls=%fused_computation.1.clone.1 | convolution fusion | flops 814743040 | bytes 14295552 | tf_op jit(solution)/shard_map/while/body/eval_jaxpr/qhd,khd->hqk/dot_general | solution.py:44
  178.3 2.9 %fusion.66 = f32[512]{0:T(512)S(1)} fusion(f32[512,6144]{1,0:T(8,128)S(1)} %get-tuple-element.222, f32[512]{0:T(512)S(1)} %broadcast_maximum_fusion.2, pred[6144]{0:T(1024)(128)(4,1)S(1)} %broadcast_compare_fusion.2), kind=kLoop, calls=%fused_computation.2.clone.1 | loop fusion | flops 12582400 | bytes 12593152 | tf_op jit(solution)/shard_map/while/body/eval_jaxpr/reduce_sum | solution.py:52
  181.3 2.2 fusion.67
  183.4 0.6 dynamic_slice.44
  187.9 0.2 fusion.65
  188.2 3.5 %select_reduce_fusion.2 = (f32[512]{0:T(512)S(1)}, f32[512,6144]{1,0:T(8,128)S(1)}) fusion(pred[6144]{0:T(1024)(128)(4,1)S(1)} %broadcast_compare_fusion.2, bf16[2,6144,1,128]{3,1,2,0:T(8,128)(2,1)} %get-tuple-element.256, bf16[4,512,1,128]{3,1,2,0:T(8,128)(2,1)S(1)} %get-tuple-element.255, s32[]{:T(128)} %get-tuple-element.237), kind=kOutput, calls=%fused_computation.1.clone.1 | convolution fusion | flops 814743040 | bytes 14295552 | tf_op jit(solution)/shard_map/while/body/eval_jaxpr/qhd,khd->hqk/dot_general | solution.py:44
  191.7 2.9 %fusion.66 = f32[512]{0:T(512)S(1)} fusion(f32[512,6144]{1,0:T(8,128)S(1)} %get-tuple-element.222, f32[512]{0:T(512)S(1)} %broadcast_maximum_fusion.2, pred[6144]{0:T(1024)(128)(4,1)S(1)} %broadcast_compare_fusion.2), kind=kLoop, calls=%fused_computation.2.clone.1 | loop fusion | flops 12582400 | bytes 12593152 | tf_op jit(solution)/shard_map/while/body/eval_jaxpr/reduce_sum | solution.py:52
  194.7 2.2 fusion.67
  196.8 0.6 dynamic_slice.44
  201.3 0.2 fusion.65
  201.6 3.5 %select_reduce_fusion.2 = (f32[512]{0:T(512)S(1)}, f32[512,6144]{1,0:T(8,128)S(1)}) fusion(pred[6144]{0:T(1024)(128)(4,1)S(1)} %broadcast_compare_fusion.2, bf16[2,6144,1,128]{3,1,2,0:T(8,128)(2,1)} %get-tuple-element.256, bf16[4,512,1,128]{3,1,2,0:T(8,128)(2,1)S(1)} %get-tuple-element.255, s32[]{:T(128)} %get-tuple-element.237), kind=kOutput, calls=%fused_computation.1.clone.1 | convolution fusion | flops 814743040 | bytes 14295552 | tf_op jit(solution)/shard_map/while/body/eval_jaxpr/qhd,khd->hqk/dot_general | solution.py:44
  205.1 2.9 %fusion.66 = f32[512]{0:T(512)S(1)} fusion(f32[512,6144]{1,0:T(8,128)S(1)} %get-tuple-element.222, f32[512]{0:T(512)S(1)} %broadcast_maximum_fusion.2, pred[6144]{0:T(1024)(128)(4,1)S(1)} %broadcast_compare_fusion.2), kind=kLoop, calls=%fused_computation.2.clone.1 | loop fusion | flops 12582400 | bytes 12593152 | tf_op jit(solution)/shard_map/while/body/eval_jaxpr/reduce_sum | solution.py:52
  208.0 2.2 fusion.67
  210.2 18.6 %all_to_all.149 = bf16[32,64,128]{2,1,0:T(8,128)(2,1)S(1)} all-to-all(bf16[32,64,128]{2,1,0:T(8,128)(2,1)S(1)} %bitcast.147), channel_id=1, replica_groups=mesh['cfg'=2,'blk'=4,'uly'=32] {'uly'}, dimensions={0} | all-to-all | bytes 1048576 | tf_op jit(solution)/shard_map/all_to_all | solution.py:131
  228.8 0.9 copy_bitcast_fusion
  (36 shorter events, 0.1 us)
Async XLA Ops:
  0.0 121.7 %copy-start = (bf16[64,4096]{1,0:T(8,128)(2,1)S(1)}, bf16[64,4096]{1,0:T(8,128)(2,1)}, u32[]{:S(2)}) copy-start(bf16[64,4096]{1,0:T(8,128)(2,1)} %param.7) | copy-start | bytes 1572868
  0.0 18.8 %copy-start.2 = (bf16[64,4096]{1,0:T(8,128)(2,1)S(1)}, bf16[64,4096]{1,0:T(8,128)(2,1)}, u32[]{:S(2)}) copy-start(bf16[64,4096]{1,0:T(8,128)(2,1)} %param.9) | copy-start | bytes 1572868
  2.1 28.8 %all-to-all-start.2 = ((bf16[64,32,128]{2,0,1:T(8,128)(2,1)}), bf16[64,32,128]{2,0,1:T(8,128)(2,1)S(1)}, u32[]{:S(2)}, u32[]{:S(2)}) async-start(bf16[64,32,128]{2,0,1:T(8,128)(2,1)} %copy_bitcast_fusion.2), calls=%async_computation.2 | async-start | bytes 1048576 | tf_op jit(solution)/shard_map/all_to_all | solution.py:80
  15.6 26.5 %collective-permute-start = (bf16[2,64,4096]{2,1,0:T(8,128)(2,1)}, bf16[2,64,4096]{2,1,0:T(8,128)(2,1)}, u32[]{:S(2)}, u32[]{:S(2)}) collective-permute-start(bf16[2,64,4096]{2,1,0:T(8,128)(2,1)} %pad_maximum_fusion), channel_id=1, source_target_pairs={{0,32},{32,64},{64,96},{1,33},{33,65},{65,97},{2,34},{34,66},{66,9... | collective-permute-start | bytes 3145736 | tf_op jit(solution)/shard_map/ppermute | solution.py:20
  30.9 21.8 %all-to-all-start.5 = ((bf16[64,32,128]{2,0,1:T(8,128)(2,1)}), bf16[64,32,128]{2,0,1:T(8,128)(2,1)S(1)}, u32[]{:S(2)}, u32[]{:S(2)}) async-start(bf16[64,32,128]{2,0,1:T(8,128)(2,1)} %copy_bitcast_fusion.1), calls=%async_computation.5 | async-start | bytes 1048576 | tf_op jit(solution)/shard_map/all_to_all | solution.py:81
  35.8 25.9 %collective-permute-start.1 = (bf16[2,64,4096]{2,1,0:T(8,128)(2,1)}, bf16[2,64,4096]{2,1,0:T(8,128)(2,1)}, u32[]{:S(2)}, u32[]{:S(2)}) collective-permute-start(bf16[2,64,4096]{2,1,0:T(8,128)(2,1)} %pad_maximum_fusion), channel_id=1, source_target_pairs={{32,0},{64,32},{96,64},{33,1},{65,33},{97,65},{34,2},{66,34},{98,6... | collective-permute-start | bytes 3145736 | tf_op jit(solution)/shard_map/ppermute | solution.py:23
  52.7 21.7 %all-to-all-start.1 = ((bf16[64,32,128]{2,0,1:T(8,128)(2,1)}), bf16[64,32,128]{2,0,1:T(8,128)(2,1)S(1)}, u32[]{:S(2)}, u32[]{:S(2)}) async-start(bf16[64,32,128]{2,0,1:T(8,128)(2,1)} %copy.54), calls=%async_computation.1 | async-start | bytes 1048576 | tf_op jit(solution)/shard_map/all_to_all | solution.py:82
  63.7 37.0 %copy-start.7 = (s32[16,12]{1,0:T(8,128)S(1)}, s32[16,12]{1,0:T(8,128)}, u32[]{:S(2)}) copy-start(s32[16,12]{1,0:T(8,128)} %param.10) | copy-start | bytes 2308
  63.7 37.1 %copy-start.8 = (s32[16]{0:T(128)S(1)}, s32[16]{0:T(128)}, u32[]{:S(2)}) copy-start(s32[16]{0:T(128)} %param.11) | copy-start | bytes 196
  74.4 48.3 %copy-start.3 = (bf16[64,32,128]{2,0,1:T(8,128)(2,1)}, bf16[64,32,128]{2,0,1:T(8,128)(2,1)S(1)}, u32[]{:S(2)}) copy-start(bf16[64,32,128]{2,0,1:T(8,128)(2,1)S(1)} %all-to-all-done.1) | copy-start | bytes 1572868
  74.4 21.5 %all-to-all-start.3 = ((bf16[64,32,128]{2,0,1:T(8,128)(2,1)}), bf16[64,32,128]{2,0,1:T(8,128)(2,1)S(1)}, u32[]{:S(2)}, u32[]{:S(2)}) async-start(bf16[64,32,128]{2,0,1:T(8,128)(2,1)} %copy.56), calls=%async_computation.3 | async-start | bytes 1048576 | tf_op jit(solution)/shard_map/all_to_all | solution.py:84
  95.9 26.8 %copy-start.4 = (bf16[64,32,128]{2,0,1:T(8,128)(2,1)}, bf16[64,32,128]{2,0,1:T(8,128)(2,1)S(1)}, u32[]{:S(2)}) copy-start(bf16[64,32,128]{2,0,1:T(8,128)(2,1)S(1)} %all-to-all-done.3) | copy-start | bytes 1572868
  95.9 20.9 %all-to-all-start.4 = ((bf16[64,32,128]{2,0,1:T(8,128)(2,1)}), bf16[64,32,128]{2,0,1:T(8,128)(2,1)S(1)}, u32[]{:S(2)}, u32[]{:S(2)}) async-start(bf16[64,32,128]{2,0,1:T(8,128)(2,1)} %copy.57), calls=%async_computation.4 | async-start | bytes 1048576 | tf_op jit(solution)/shard_map/all_to_all | solution.py:83
  116.7 5.9 %copy-start.5 = (bf16[64,32,128]{2,0,1:T(8,128)(2,1)}, bf16[64,32,128]{2,0,1:T(8,128)(2,1)S(1)}, u32[]{:S(2)}) copy-start(bf16[64,32,128]{2,0,1:T(8,128)(2,1)S(1)} %all-to-all-done.4) | copy-start | bytes 1572868
  116.7 20.2 %all-to-all-start.6 = ((bf16[64,32,128]{2,0,1:T(8,128)(2,1)}), bf16[64,32,128]{2,0,1:T(8,128)(2,1)}, u32[]{:S(2)}, u32[]{:S(2)}) async-start(bf16[64,32,128]{2,0,1:T(8,128)(2,1)} %copy.59), calls=%async_computation.6 | async-start | bytes 1048576 | tf_op jit(solution)/shard_map/all_to_all | solution.py:85
  137.0 19.7 %all-to-all-start = ((bf16[64,32,128]{2,0,1:T(8,128)(2,1)}), bf16[64,32,128]{2,0,1:T(8,128)(2,1)S(1)}, u32[]{:S(2)}, u32[]{:S(2)}) async-start(bf16[64,32,128]{2,0,1:T(8,128)(2,1)} %copy_bitcast_fusion.3), calls=%async_computation | async-start | bytes 1048576 | tf_op jit(solution)/shard_map/all_to_all | solution.py:79
  143.2 13.5 %copy-start.6 = (bf16[4,512,1,128]{3,1,2,0:T(8,128)(2,1)S(1)}, bf16[4,512,1,128]{3,1,2,0:T(8,128)(2,1)}, u32[]{:S(2)}) copy-start(bf16[4,512,1,128]{3,1,2,0:T(8,128)(2,1)} %custom-call) | copy-start | bytes 1572868
  164.9 2.9 %copy-start.1 = (bf16[2,6144,1,128]{3,1,2,0:T(8,128)(2,1)S(1)}, bf16[2,6144,1,128]{3,1,2,0:T(8,128)(2,1)}, u32[]{:S(2)}) copy-start(bf16[2,6144,1,128]{3,1,2,0:T(8,128)(2,1)} %get-tuple-element.256) | copy-start | bytes 9437188 | tf_op jit(solution)/shard_map/while
  178.3 2.9 %copy-start.1 = (bf16[2,6144,1,128]{3,1,2,0:T(8,128)(2,1)S(1)}, bf16[2,6144,1,128]{3,1,2,0:T(8,128)(2,1)}, u32[]{:S(2)}) copy-start(bf16[2,6144,1,128]{3,1,2,0:T(8,128)(2,1)} %get-tuple-element.256) | copy-start | bytes 9437188 | tf_op jit(solution)/shard_map/while
  191.7 2.9 %copy-start.1 = (bf16[2,6144,1,128]{3,1,2,0:T(8,128)(2,1)S(1)}, bf16[2,6144,1,128]{3,1,2,0:T(8,128)(2,1)}, u32[]{:S(2)}) copy-start(bf16[2,6144,1,128]{3,1,2,0:T(8,128)(2,1)} %get-tuple-element.256) | copy-start | bytes 9437188 | tf_op jit(solution)/shard_map/while
  205.1 2.9 %copy-start.1 = (bf16[2,6144,1,128]{3,1,2,0:T(8,128)(2,1)S(1)}, bf16[2,6144,1,128]{3,1,2,0:T(8,128)(2,1)}, u32[]{:S(2)}) copy-start(bf16[2,6144,1,128]{3,1,2,0:T(8,128)(2,1)} %get-tuple-element.256) | copy-start | bytes 9437188 | tf_op jit(solution)/shard_map/while
where the time goes:
time: 232 us; the launch traced here: 230 us
  waiting for transfers between devices  90.7 us (39%)
  starting transfers between devices  45.9 us (20%)
  matrix products  23.6 us (10%)
  other arithmetic  18.7 us (8%)
  blocking collectives  18.6 us (8%)
  local copies, waits for them, and re-layouts  16.1 us (7%)
  loops' own time  15.8 us (7%)
    all_to_all x1, blocking collectives, body(): lax.all_to_all(attended_block, 'uly', split_axis=0, concat_axis=1, tiled=...  18.6 us
    another operation x1, loops' own time, body(): lax.map(one_tile, (jnp.arange(tiles_here, dtype=jnp.int32), query_tiles))  15.8 us
    all_to_all x1, waiting for transfers between devices, body(): lax.all_to_all(key_upper, 'uly', split_axis=1, concat_axis=0, tiled=True)  15.5 us
    dot_general x4, matrix products, absorb(): jnp.einsum('qhd,khd->hqk', query_tile, key_piece, preferred_element_type=...  14.1 us
    all_to_all x1, waiting for transfers between devices, body(): lax.all_to_all(value_lower, 'uly', split_axis=1, concat_axis=0, tiled=True)  13.6 us
    all_to_all x1, waiting for transfers between devices, body(): lax.all_to_all(value_upper, 'uly', split_axis=1, concat_axis=0, tiled=True)  13 us
    reduce_sum x4, other arithmetic, absorb(): row_total = jnp.sum(weights, axis=-1)  11.7 us
    all_to_all x1, waiting for transfers between devices, body(): lax.all_to_all(queries, 'uly', split_axis=1, concat_axis=0, tiled=True)  11.6 us
  transfers between devices with their start and end apart: 9, of which 9 were waited for; matrix products, arithmetic and copies ran while one was open for 8% of the time, Pallas kernels for 0%

commit v1 on v0

v1 whole, which is shorter than its diff:
```python
import math

import jax
import jax.numpy as jnp
from jax import lax
from jax.experimental import pallas as pl
from jax.experimental.pallas import tpu as pltpu
from jax.sharding import PartitionSpec as P

HD=128; TILE=512
C = HD ** -0.5 * math.log2(math.e)
F32=jnp.float32; BF=jnp.bfloat16

def attn_kernel(tl, used, blk, q_hbm, low_hbm, own_hbm, high_hbm, o_ref, kv, qv, S, mx, acc, sems):
    b = blk[0]
    cps=[pltpu.make_async_copy(q_hbm, qv, sems.at[0]),
         pltpu.make_async_copy(low_hbm, kv.at[pl.ds(0,32)], sems.at[1]),
         pltpu.make_async_copy(own_hbm, kv.at[pl.ds(32,32)], sems.at[2]),
         pltpu.make_async_copy(high_hbm, kv.at[pl.ds(64,32)], sems.at[3])]
    for c in cps: c.start()
    for c in cps: c.wait()
    def tile(i, _):
        g = 4*b + i
        n = used[g]
        q = qv[pl.ds(8*i, 8)].reshape(TILE, HD)
        mx[...] = jnp.full(mx.shape, -3e38, F32)
        def p1(s, _):
            t = tl[g, s] - 4*b + 4
            k = kv[pl.ds(8*t, 8), 0].reshape(TILE, HD)
            sc = lax.dot_general(q, k, (((1,),(1,)),((),())), preferred_element_type=F32)
            S[s] = sc
            m = jnp.maximum(jnp.maximum(sc[:, :128], sc[:, 128:256]), jnp.maximum(sc[:, 256:384], sc[:, 384:]))
            mx[...] = jnp.maximum(mx[...], m)
            return 0
        lax.fori_loop(0, n, p1, 0)
        mx[...] = jnp.broadcast_to(jnp.max(mx[...], axis=1, keepdims=True) * C, mx.shape)
        acc[...] = jnp.zeros_like(acc)
        def p2(s, _):
            t = tl[g, s] - 4*b + 4
            v = kv[pl.ds(8*t, 8), 1].reshape(TILE, HD)
            vx = jnp.concatenate([v, jnp.ones_like(v)], axis=1)
            m = mx[...]
            p = jnp.concatenate([jnp.exp2(S[s, :, 128*j:128*(j+1)] * C - m).astype(BF) for j in range(4)], axis=1)
            acc[...] += jnp.dot(p, vx, preferred_element_type=F32)
            return 0
        lax.fori_loop(0, n, p2, 0)
        o_ref[pl.ds(8*i, 8)] = (acc[:, :128] / acc[:, 128:]).astype(BF).reshape(8, 64, HD)
        return 0
    lax.fori_loop(0, 4, tile, 0)

def attention(tl, used, blk, q, low, own, high):
    anyspec = pl.BlockSpec(memory_space=pl.ANY)
    return pl.pallas_call(
        attn_kernel,
        grid_spec=pltpu.PrefetchScalarGridSpec(
            num_scalar_prefetch=3, grid=(1,),
            in_specs=[anyspec]*4,
            out_specs=pl.BlockSpec((32,64,HD), lambda i,*_: (0,0,0)),
            scratch_shapes=[pltpu.VMEM((96,2,64,HD),BF), pltpu.VMEM((32,64,HD),BF), pltpu.VMEM((12,TILE,TILE),F32),
                            pltpu.VMEM((TILE,128),F32), pltpu.VMEM((TILE,256),F32), pltpu.SemaphoreType.DMA((4,))]),
        out_shape=jax.ShapeDtypeStruct((32,64,HD),BF),
        compiler_params=pltpu.CompilerParams(vmem_limit_bytes=48*2**20),
        cost_estimate=pl.CostEstimate(flops=32*2*2*512*512*128, bytes_accessed=4*2**20, transcendentals=32*512*512),
    )(tl, used, blk, q, low, own, high)

def heads_first(x):
    return jnp.transpose(x.reshape(x.shape[0], -1, HD), (1, 0, 2))


def exchange(x):
    return lax.all_to_all(x, "uly", split_axis=0, concat_axis=0, tiled=True)


def body(queries, key_states, value_states, tile_list, tile_used):
    blk = lax.axis_index("blk").astype(jnp.int32).reshape(1)
    count = lax.axis_size("blk")
    up = [(i, i + 1) for i in range(count - 1)]
    down = [(i + 1, i) for i in range(count - 1)]
    kv = exchange(jnp.stack([heads_first(key_states), heads_first(value_states)], axis=1))
    q = heads_first(queries)
    kv, q = lax.optimization_barrier((kv, q))
    low = lax.ppermute(kv, "blk", up)
    high = lax.ppermute(kv, "blk", down)
    q = exchange(q)
    out = attention(tile_list, tile_used, blk, q, low, kv, high)
    out = exchange(out)
    return jnp.transpose(out, (1, 0, 2)).reshape(queries.shape)


def solution(mesh):
    spec = P(("cfg", "blk", "uly"), None)
    return jax.shard_map(
        body,
        mesh=mesh,
        in_specs=(spec, spec, spec, P(), P()),
        out_specs=spec,
        check_vma=False,
    )
```

time: 232 us -> 116 us (0.50)
  waiting for transfers between devices: 90.7 us -> 44.1 us
  matrix products: 23.6 us -> 0 us
  starting transfers between devices: 45.9 us -> 22.4 us
  Pallas kernels: 0 us -> 21.4 us
  other arithmetic: 18.7 us -> 1.07 us
  loops' own time: 15.8 us -> 0 us
  local copies, waits for them, and re-layouts: 16.1 us -> 4.18 us
  blocking collectives: 18.6 us -> 22.4 us
    all_to_all x7 -> x2, waiting for transfers between devices: 82.7 us -> 44.1 us  [exchange(): return lax.all_to_all(x, 'uly', split_axis=0, concat_axis=0, tiled=True)]
    all_to_all x7 -> x2, starting transfers between devices: 40.4 us -> 16.5 us  [exchange(): return lax.all_to_all(x, 'uly', split_axis=0, concat_axis=0, tiled=True)]
    dot_general x12 -> x0, matrix products: 23.6 us -> none  [the longest x4 14.1 us: absorb(): jnp.einsum('qhd,khd->hqk', query_tile, key_piece, preferred_element_type=...]
    pallas_call x0 -> x1, Pallas kernels: none -> 21.4 us  [attention(): pl.pallas_call(attn_kernel, grid_spec=pltpu.PrefetchScalarGridSpec(num_sc...]
    another operation x1 -> x0, loops' own time: 15.8 us -> none  [body(): lax.map(one_tile, (jnp.arange(tiles_here, dtype=jnp.int32), query_tiles))]
    reduce_sum x4 -> x0, other arithmetic: 11.7 us -> none  [absorb(): row_total = jnp.sum(weights, axis=-1)]
    all_to_all x8 -> x0, local copies, waits for them, and re-layouts: 8.88 us -> none  [the longest x1 2.09 us: body(): lax.all_to_all(key_states, 'uly', split_axis=1, concat_axis=0, tiled=True)]
    ppermute x2, waiting for transfers between devices: 8.04 us -> 0.01 us  [the longest x1 0.01 us: body(): high = lax.ppermute(kv, 'blk', down)]
  transfers between devices with their start and end apart: 9 -> 4, of which waited for: 9 -> 2; matrix products, arithmetic and copies ran while one was open for 8% -> 1% of each run, Pallas kernels for 0% -> 0%
where the time goes in v1:
time: 116 us
  waiting for transfers between devices  44.1 us (38%)
  starting transfers between devices  22.4 us (19%)
  blocking collectives  22.4 us (19%)
  Pallas kernels  21.4 us (18%)
  local copies, waits for them, and re-layouts  4.18 us (4%)
    all_to_all x2, waiting for transfers between devices, exchange(): return lax.all_to_all(x, 'uly', split_axis=0, concat_axis=0, tiled=True)  44.1 us
    all_to_all x1, blocking collectives, exchange(): return lax.all_to_all(x, 'uly', split_axis=0, concat_axis=0, tiled=True)  22.4 us
    pallas_call x1, Pallas kernels, attention(): pl.pallas_call(attn_kernel, grid_spec=pltpu.PrefetchScalarGridSpec(num_sc...  21.4 us
    all_to_all x2, starting transfers between devices, exchange(): return lax.all_to_all(x, 'uly', split_axis=0, concat_axis=0, tiled=True)  16.5 us
    ppermute x1, starting transfers between devices, body(): low = lax.ppermute(kv, 'blk', up)  3.55 us
    ppermute x1, starting transfers between devices, body(): high = lax.ppermute(kv, 'blk', down)  2.35 us
  transfers between devices with their start and end apart: 4, of which 2 were waited for; matrix products, arithmetic and copies ran while one was open for 1% of the time, Pallas kernels for 0%

profile of v1, /device:TPU:48, one launch (start us, length us, event | category | flops | bytes accessed | tf_op | source)
XLA Modules:
  0.0 115.7 jit_solution(5693043996929623409)
XLA Ops:
  0.0 0.0 copy-start
  0.0 1.0 copy-done
  1.0 1.3 %bitcast_bitcast_fusion.1 = (bf16[32,1,64,128]{3,2,1,0:T(8,128)(2,1)S(1)}, bf16[32,1,64,128]{3,2,1,0:T(8,128)(2,1)S(1)}) fusion(bf16[64,4096]{1,0:T(8,128)(2,1)S(1)} %copy-done, bf16[64,4096]{1,0:T(8,128)(2,1)} %param.7), kind=kLoop, calls=%fused_computation.3 | loop fusion | bytes 2097152 | tf_op jit(solution)/shard_map/stack | solution.py:79
  2.4 1.1 pad_maximum_fusion
  3.4 0.0 copy-start.3
  3.5 11.3 %all-to-all-start = ((bf16[32,2,64,128]{3,2,1,0:T(8,128)(2,1)}), bf16[32,2,64,128]{3,2,1,0:T(8,128)(2,1)S(1)}, u32[]{:S(2)}, u32[]{:S(2)}) async-start(bf16[32,2,64,128]{3,2,1,0:T(8,128)(2,1)} %pad_maximum_fusion), calls=%async_computation | async-start | bytes 2097152 | tf_op jit(solution)/shard_map/all_to_all | solution.py:71
  14.8 0.0 copy-done.3
  14.8 0.9 bitcast_bitcast_fusion
  15.7 27.6 %all-to-all-done.own_hbm = bf16[32,2,64,128]{3,2,1,0:T(8,128)(2,1)S(1)} async-done(((bf16[32,2,64,128]{3,2,1,0:T(8,128)(2,1)}), bf16[32,2,64,128]{3,2,1,0:T(8,128)(2,1)S(1)}, u32[]{:S(2)}, u32[]{:S(2)}) %all-to-all-start) | async-done | bytes 1048608 | tf_op jit(solution)/shard_map/all_to_all | solution.py:71
  43.3 2.3 %collective-permute-start.1 = (bf16[32,2,64,128]{3,2,1,0:T(8,128)(2,1)S(1)}, bf16[32,2,64,128]{3,2,1,0:T(8,128)(2,1)S(1)}, u32[]{:S(2)}, u32[]{:S(2)}) collective-permute-start(bf16[32,2,64,128]{3,2,1,0:T(8,128)(2,1)S(1)} %all-to-all-done.own_hbm), channel_id=1, source_target_pairs={{32,0},{64,32},{96,64},{33,1},{65,33},{97,65},{34,2},{66,34},{98,6... | collective-permute-start | bytes 3145736 | tf_op jit(solution)/shard_map/ppermute | solution.py:83
  45.7 3.5 %collective-permute-start = (bf16[32,2,64,128]{3,2,1,0:T(8,128)(2,1)S(1)}, bf16[32,2,64,128]{3,2,1,0:T(8,128)(2,1)}, u32[]{:S(2)}, u32[]{:S(2)}) collective-permute-start(bf16[32,2,64,128]{3,2,1,0:T(8,128)(2,1)S(1)} %all-to-all-done.own_hbm), channel_id=1, source_target_pairs={{0,32},{32,64},{64,96},{1,33},{33,65},{65,97},{2,34},{34,66},{66,9... | collective-permute-start | bytes 3145736 | tf_op jit(solution)/shard_map/ppermute | solution.py:82
  49.2 5.2 %all-to-all-start.1 = ((bf16[32,64,128]{2,1,0:T(8,128)(2,1)}), bf16[32,64,128]{2,1,0:T(8,128)(2,1)S(1)}, u32[]{:S(2)}, u32[]{:S(2)}) async-start(bf16[32,64,128]{2,1,0:T(8,128)(2,1)} %bitcast_bitcast_fusion), calls=%async_computation.1 | async-start | bytes 1048576 | tf_op jit(solution)/shard_map/all_to_all | solution.py:71
  54.4 0.0 copy-start.1
  54.4 0.0 copy-start.2
  54.4 16.5 %all-to-all-done.1.q_hbm = bf16[32,64,128]{2,1,0:T(8,128)(2,1)S(1)} async-done(((bf16[32,64,128]{2,1,0:T(8,128)(2,1)}), bf16[32,64,128]{2,1,0:T(8,128)(2,1)S(1)}, u32[]{:S(2)}, u32[]{:S(2)}) %all-to-all-start.1) | async-done | bytes 524320 | tf_op jit(solution)/shard_map/all_to_all | solution.py:71
  71.0 0.0 collective-permute-done.1.high_hbm
  71.0 0.0 collective-permute-done.low_hbm
  71.0 0.0 copy-done.1
  71.0 0.0 copy-done.2
  71.0 21.4 %shard_map.55 = bf16[32,64,128]{2,1,0:T(8,128)(2,1)S(1)} custom-call(s32[16,12]{1,0:T(8,128)S(1)} %copy-done.1, s32[16]{0:T(128)S(1)} %copy-done.2, s32[1]{0:T(128)} %bitcast.blk, bf16[32,64,128]{2,1,0:T(8,128)(2,1)S(1)} %all-to-all-done.1.q_hbm, bf16[32,2,64,128]{3,2,1,0:T(8,128)(2,1)} %collective-permute-done.low_hbm, ...), custom_call_target="tpu_custom_call" | custom-call | flops 4294967296 | bytes 4194304 | tf_op jit(solution)/shard_map/pallas_call | solution.py:53
  92.4 22.4 %all_to_all.15 = bf16[32,64,128]{2,1,0:T(8,128)(2,1)S(1)} all-to-all(bf16[32,64,128]{2,1,0:T(8,128)(2,1)S(1)} %shard_map.55), channel_id=1, replica_groups=mesh['cfg'=2,'blk'=4,'uly'=32] {'uly'}, dimensions={0} | all-to-all | bytes 1048576 | tf_op jit(solution)/shard_map/all_to_all | solution.py:71
  114.8 0.9 copy_bitcast_fusion
Async XLA Ops:
  0.0 1.0 copy-start
  3.4 11.3 %copy-start.3 = (bf16[64,4096]{1,0:T(8,128)(2,1)S(1)}, bf16[64,4096]{1,0:T(8,128)(2,1)}, u32[]{:S(2)}) copy-start(bf16[64,4096]{1,0:T(8,128)(2,1)} %param.5) | copy-start | bytes 1572868
  3.5 39.9 %all-to-all-start = ((bf16[32,2,64,128]{3,2,1,0:T(8,128)(2,1)}), bf16[32,2,64,128]{3,2,1,0:T(8,128)(2,1)S(1)}, u32[]{:S(2)}, u32[]{:S(2)}) async-start(bf16[32,2,64,128]{3,2,1,0:T(8,128)(2,1)} %pad_maximum_fusion), calls=%async_computation | async-start | bytes 2097152 | tf_op jit(solution)/shard_map/all_to_all | solution.py:71
  43.3 27.7 %collective-permute-start.1 = (bf16[32,2,64,128]{3,2,1,0:T(8,128)(2,1)S(1)}, bf16[32,2,64,128]{3,2,1,0:T(8,128)(2,1)S(1)}, u32[]{:S(2)}, u32[]{:S(2)}) collective-permute-start(bf16[32,2,64,128]{3,2,1,0:T(8,128)(2,1)S(1)} %all-to-all-done.own_hbm), channel_id=1, source_target_pairs={{32,0},{64,32},{96,64},{33,1},{65,33},{97,65},{34,2},{66,34},{98,6... | collective-permute-start | bytes 3145736 | tf_op jit(solution)/shard_map/ppermute | solution.py:83
  45.7 25.3 %collective-permute-start = (bf16[32,2,64,128]{3,2,1,0:T(8,128)(2,1)S(1)}, bf16[32,2,64,128]{3,2,1,0:T(8,128)(2,1)}, u32[]{:S(2)}, u32[]{:S(2)}) collective-permute-start(bf16[32,2,64,128]{3,2,1,0:T(8,128)(2,1)S(1)} %all-to-all-done.own_hbm), channel_id=1, source_target_pairs={{0,32},{32,64},{64,96},{1,33},{33,65},{65,97},{2,34},{34,66},{66,9... | collective-permute-start | bytes 3145736 | tf_op jit(solution)/shard_map/ppermute | solution.py:82
  49.2 21.8 %all-to-all-start.1 = ((bf16[32,64,128]{2,1,0:T(8,128)(2,1)}), bf16[32,64,128]{2,1,0:T(8,128)(2,1)S(1)}, u32[]{:S(2)}, u32[]{:S(2)}) async-start(bf16[32,64,128]{2,1,0:T(8,128)(2,1)} %bitcast_bitcast_fusion), calls=%async_computation.1 | async-start | bytes 1048576 | tf_op jit(solution)/shard_map/all_to_all | solution.py:71
  54.4 16.6 %copy-start.1 = (s32[16,12]{1,0:T(8,128)S(1)}, s32[16,12]{1,0:T(8,128)}, u32[]{:S(2)}) copy-start(s32[16,12]{1,0:T(8,128)} %tl.1) | copy-start | bytes 2308
  54.4 16.6 %copy-start.2 = (s32[16]{0:T(128)S(1)}, s32[16]{0:T(128)}, u32[]{:S(2)}) copy-start(s32[16]{0:T(128)} %used.1) | copy-start | bytes 196

commit v2 on v1

v2 whole, which is shorter than its diff:
```python
import math

import jax
import jax.numpy as jnp
from jax import lax
from jax.experimental import pallas as pl
from jax.experimental.pallas import tpu as pltpu
from jax.sharding import PartitionSpec as P

HD=128; TILE=512
U=4
GROUP=2
SLOTS=12*GROUP+U
C = HD ** -0.5 * math.log2(math.e)
F32=jnp.float32; BF=jnp.bfloat16

def attn_kernel(tl, used, blk, q_hbm, low_hbm, own_hbm, high_hbm, o_ref, kv, qv, S, mx, acc, it, iq, ia, sems):
    b = blk[0]
    regions = (low_hbm, own_hbm, high_hbm)
    q_copy = pltpu.make_async_copy(q_hbm, qv, sems.at[0])
    k_copies = [pltpu.make_async_copy(r.at[:, 0], kv.at[0, pl.ds(32*j, 32)], sems.at[1+j]) for j, r in enumerate(regions)]
    v_copies = [pltpu.make_async_copy(r.at[:, 1], kv.at[1, pl.ds(32*j, 32)], sems.at[4+j]) for j, r in enumerate(regions)]
    for c in [q_copy] + k_copies + v_copies:
        c.start()
    for grp in range(4//GROUP):
        f = jnp.int32(0)
        for a in range(GROUP):
            g = 4*b + grp*GROUP + a
            def put(s, f):
                it[f] = tl[g, s] - 4*b + 4
                iq[f] = jnp.int32(grp*GROUP + a)
                ia[f] = jnp.int32(a)
                return f + 1
            f = lax.fori_loop(0, used[g], put, f)
        for j in range(U-1):
            it[f+j] = jnp.int32(4)
            iq[f+j] = jnp.int32(0)
            ia[f+j] = jnp.int32(GROUP)
        trips = (f + (U-1)) // U
        mx[...] = jnp.full(mx.shape, -3e38, F32)
        acc[...] = jnp.zeros_like(acc)
        def p1(c, _):
            for j in range(U):
                s = c*U + j
                q = qv[pl.ds(8*iq[s], 8)].reshape(TILE, HD)
                k = kv[0, pl.ds(8*it[s], 8)].reshape(TILE, HD)
                sc = lax.dot_general(q, k, (((1,),(1,)),((),())), preferred_element_type=F32)
                S[s] = sc
                m = jnp.maximum(jnp.maximum(sc[:, :128], sc[:, 128:256]), jnp.maximum(sc[:, 256:384], sc[:, 384:]))
                mx[ia[s]] = jnp.maximum(mx[ia[s]], m)
            return 0
        if grp == 0:
            for c in [q_copy] + k_copies:
                c.wait()
        lax.fori_loop(0, trips, p1, 0)
        for a in range(GROUP):
            mx[a] = jnp.broadcast_to(jnp.max(mx[a], axis=1, keepdims=True) * C, (TILE,128))
        def p2(c, _):
            for j in range(U):
                s = c*U + j
                v = kv[1, pl.ds(8*it[s], 8)].reshape(TILE, HD)
                vx = jnp.concatenate([v, jnp.ones_like(v)], axis=1)
                m = mx[ia[s]]
                p = jnp.concatenate([jnp.exp2(S[s, :, 128*j:128*(j+1)] * C - m).astype(BF) for j in range(4)], axis=1)
                acc[ia[s]] += jnp.dot(p, vx, preferred_element_type=F32)
            return 0
        if grp == 0:
            for c in v_copies:
                c.wait()
        lax.fori_loop(0, trips, p2, 0)
        for a in range(GROUP):
            i = grp*GROUP + a
            o_ref[pl.ds(8*i, 8)] = (acc[a, :, :128] / acc[a, :, 128:]).astype(BF).reshape(8, 64, HD)

def attention(tl, used, blk, q, low, own, high):
    anyspec = pl.BlockSpec(memory_space=pl.ANY)
    return pl.pallas_call(
        attn_kernel,
        grid_spec=pltpu.PrefetchScalarGridSpec(
            num_scalar_prefetch=3, grid=(1,),
            in_specs=[anyspec]*4,
            out_specs=pl.BlockSpec((32,64,HD), lambda i,*_: (0,0,0)),
            scratch_shapes=[pltpu.VMEM((2,96,64,HD),BF), pltpu.VMEM((32,64,HD),BF), pltpu.VMEM((SLOTS,TILE,TILE),F32),
                            pltpu.VMEM((GROUP+1,TILE,128),F32), pltpu.VMEM((GROUP+1,TILE,256),F32),
                            pltpu.SMEM((SLOTS,),jnp.int32),pltpu.SMEM((SLOTS,),jnp.int32),pltpu.SMEM((SLOTS,),jnp.int32),
                            pltpu.SemaphoreType.DMA((7,))]),
        out_shape=jax.ShapeDtypeStruct((32,64,HD),BF),
        compiler_params=pltpu.CompilerParams(vmem_limit_bytes=38*2**20),
        cost_estimate=pl.CostEstimate(flops=32*2*2*512*512*128, bytes_accessed=4*2**20, transcendentals=32*512*512),
    )(tl, used, blk, q, low, own, high)

def pack_kernel(*refs):
    ins, out = refs[:-1], refs[-1]
    for h in range(out.shape[0]):
        for a, r in enumerate(ins):
            piece = r[:, HD * h : HD * (h + 1)]
            if len(ins) > 1:
                out[h, a] = piece
            else:
                out[h] = piece


def pack(*arrays):
    rows, width = arrays[0].shape
    heads = width // HD
    steps = 2
    inner = (len(arrays), rows, HD) if len(arrays) > 1 else (rows, HD)
    nbytes = 2 * len(arrays) * rows * width * 2
    return pl.pallas_call(
        pack_kernel,
        grid=(steps,),
        in_specs=[pl.BlockSpec((rows, width // steps), lambda i: (0, i))] * len(arrays),
        out_specs=pl.BlockSpec((heads // steps,) + inner, lambda i: (i,) + (0,) * len(inner)),
        out_shape=jax.ShapeDtypeStruct((heads,) + inner, arrays[0].dtype),
        cost_estimate=pl.CostEstimate(flops=0, bytes_accessed=nbytes, transcendentals=0),
    )(*arrays)


def exchange(x):
    return lax.all_to_all(x, "uly", split_axis=0, concat_axis=0, tiled=True)


def body(queries, key_states, value_states, tile_list, tile_used):
    blk = lax.axis_index("blk").astype(jnp.int32).reshape(1)
    count = lax.axis_size("blk")
    up = [(i, (i + 1) % count) for i in range(count)]
    down = [((i + 1) % count, i) for i in range(count)]
    kv = exchange(pack(key_states, value_states))
    q = pack(queries)
    kv, q = lax.optimization_barrier((kv, q))
    low = lax.ppermute(kv, "blk", up)
    high = lax.ppermute(kv, "blk", down)
    q = exchange(q)
    out = attention(tile_list, tile_used, blk, q, low, kv, high)
    out = exchange(out)
    return jnp.transpose(out, (1, 0, 2)).reshape(queries.shape)


def solution(mesh):
    spec = P(("cfg", "blk", "uly"), None)
    return jax.shard_map(
        body,
        mesh=mesh,
        in_specs=(spec, spec, spec, P(), P()),
        out_specs=spec,
        check_vma=False,
    )
```

time: 116 us -> 107 us (0.922)
  starting transfers between devices: 22.4 us -> 18.4 us
  local copies, waits for them, and re-layouts: 4.18 us -> 0.87 us
    pallas_call x0 -> x2, Pallas kernels: none -> 3.89 us  [pack(): pl.pallas_call(pack_kernel, grid=(steps,), in_specs=[pl.BlockSpec((rows,...]
    pallas_call x1, Pallas kernels: 21.4 us -> 18 us  [attention(): pl.pallas_call(attn_kernel, grid_spec=pltpu.PrefetchScalarGridSpec(num_sc...]
    ppermute x1, starting transfers between devices: 3.55 us -> 1.58 us  [body(): low = lax.ppermute(kv, 'blk', up)]
    ppermute x1, starting transfers between devices: 2.35 us -> 0.45 us  [body(): high = lax.ppermute(kv, 'blk', down)]
    another operation x1 -> x0, local copies, waits for them, and re-layouts: 1.32 us -> none  [body(): jnp.stack([heads_first(key_states), heads_first(value_states)], axis=1)]
  transfers between devices with their start and end apart: 4 -> 4, of which waited for: 2 -> 2; matrix products, arithmetic and copies ran while one was open for 1% -> 0% of each run, Pallas kernels for 0% -> 2%
where the time goes in v2:
time: 107 us
  waiting for transfers between devices  43.3 us (40%)
  blocking collectives  22.6 us (21%)
  Pallas kernels  21.9 us (20%)
  starting transfers between devices  18.4 us (17%)
    all_to_all x2, waiting for transfers between devices, exchange(): return lax.all_to_all(x, 'uly', split_axis=0, concat_axis=0, tiled=True)  43.3 us
    all_to_all x1, blocking collectives, exchange(): return lax.all_to_all(x, 'uly', split_axis=0, concat_axis=0, tiled=True)  22.6 us
    pallas_call x1, Pallas kernels, attention(): pl.pallas_call(attn_kernel, grid_spec=pltpu.PrefetchScalarGridSpec(num_sc...  18 us
    all_to_all x2, starting transfers between devices, exchange(): return lax.all_to_all(x, 'uly', split_axis=0, concat_axis=0, tiled=True)  16.4 us
    pallas_call x2, Pallas kernels, pack(): pl.pallas_call(pack_kernel, grid=(steps,), in_specs=[pl.BlockSpec((rows,...  3.89 us
  transfers between devices with their start and end apart: 4, of which 2 were waited for; matrix products, arithmetic and copies ran while one was open for 0% of the time, Pallas kernels for 2%

profile of v2, /device:TPU:48, one launch (start us, length us, event | category | flops | bytes accessed | tf_op | source)
XLA Modules:
  0.0 107.2 jit_solution(15994862597309102776)
XLA Ops:
  0.0 2.1 %shard_map.55 = bf16[32,2,64,128]{3,2,1,0:T(8,128)(2,1)} custom-call(bf16[64,4096]{1,0:T(8,128)(2,1)} %refs_0_.2, bf16[64,4096]{1,0:T(8,128)(2,1)} %refs_1_.1), custom_call_target="tpu_custom_call" | custom-call | bytes 2097152 | tf_op jit(solution)/shard_map/pallas_call | solution.py:109
  2.1 11.2 %all-to-all-start = ((bf16[32,2,64,128]{3,2,1,0:T(8,128)(2,1)}), bf16[32,2,64,128]{3,2,1,0:T(8,128)(2,1)S(1)}, u32[]{:S(2)}, u32[]{:S(2)}) async-start(bf16[32,2,64,128]{3,2,1,0:T(8,128)(2,1)} %shard_map.55), calls=%async_computation | async-start | bytes 2097152 | tf_op jit(solution)/shard_map/all_to_all | solution.py:120
  13.3 1.8 %shard_map.56 = bf16[32,64,128]{2,1,0:T(8,128)(2,1)} custom-call(bf16[64,4096]{1,0:T(8,128)(2,1)} %refs_0_.3), custom_call_target="tpu_custom_call" | custom-call | bytes 1048576 | tf_op jit(solution)/shard_map/pallas_call | solution.py:109
  15.1 26.7 %all-to-all-done.own_hbm = bf16[32,2,64,128]{3,2,1,0:T(8,128)(2,1)S(1)} async-done(((bf16[32,2,64,128]{3,2,1,0:T(8,128)(2,1)}), bf16[32,2,64,128]{3,2,1,0:T(8,128)(2,1)S(1)}, u32[]{:S(2)}, u32[]{:S(2)}) %all-to-all-start) | async-done | bytes 1048608 | tf_op jit(solution)/shard_map/all_to_all | solution.py:120
  41.8 0.4 collective-permute-start.1
  42.3 1.6 %collective-permute-start = (bf16[32,2,64,128]{3,2,1,0:T(8,128)(2,1)S(1)}, bf16[32,2,64,128]{3,2,1,0:T(8,128)(2,1)}, u32[]{:S(2)}, u32[]{:S(2)}) collective-permute-start(bf16[32,2,64,128]{3,2,1,0:T(8,128)(2,1)S(1)} %all-to-all-done.own_hbm), channel_id=1, source_target_pairs={{0,32},{32,64},{64,96},{96,0},{1,33},{33,65},{65,97},{97,1},{2,34}... | collective-permute-start | bytes 3145736 | tf_op jit(solution)/shard_map/ppermute | solution.py:131
  43.8 5.2 %all-to-all-start.1 = ((bf16[32,64,128]{2,1,0:T(8,128)(2,1)}), bf16[32,64,128]{2,1,0:T(8,128)(2,1)S(1)}, u32[]{:S(2)}, u32[]{:S(2)}) async-start(bf16[32,64,128]{2,1,0:T(8,128)(2,1)} %shard_map.56), calls=%async_computation.1 | async-start | bytes 1048576 | tf_op jit(solution)/shard_map/all_to_all | solution.py:120
  49.0 0.0 copy-start
  49.1 0.0 copy-start.1
  49.1 16.5 %all-to-all-done.1.q_hbm = bf16[32,64,128]{2,1,0:T(8,128)(2,1)S(1)} async-done(((bf16[32,64,128]{2,1,0:T(8,128)(2,1)}), bf16[32,64,128]{2,1,0:T(8,128)(2,1)S(1)}, u32[]{:S(2)}, u32[]{:S(2)}) %all-to-all-start.1) | async-done | bytes 524320 | tf_op jit(solution)/shard_map/all_to_all | solution.py:120
  65.6 0.0 collective-permute-done.1.high_hbm
  65.6 0.0 collective-permute-done.low_hbm
  65.6 0.0 copy-done
  65.6 0.0 copy-done.1
  65.6 18.0 %shard_map.57 = bf16[32,64,128]{2,1,0:T(8,128)(2,1)S(1)} custom-call(s32[16,12]{1,0:T(8,128)S(1)} %copy-done, s32[16]{0:T(128)S(1)} %copy-done.1, s32[1]{0:T(128)} %bitcast.blk, bf16[32,64,128]{2,1,0:T(8,128)(2,1)S(1)} %all-to-all-done.1.q_hbm, bf16[32,2,64,128]{3,2,1,0:T(8,128)(2,1)} %collective-permute-done.low_hbm, ...), custom_call_target="tpu_custom_call" | custom-call | flops 4294967296 | bytes 4194304 | tf_op jit(solution)/shard_map/pallas_call | solution.py:77
  83.7 22.6 %all_to_all.15 = bf16[32,64,128]{2,1,0:T(8,128)(2,1)S(1)} all-to-all(bf16[32,64,128]{2,1,0:T(8,128)(2,1)S(1)} %shard_map.57), channel_id=1, replica_groups=mesh['cfg'=2,'blk'=4,'uly'=32] {'uly'}, dimensions={0} | all-to-all | bytes 1048576 | tf_op jit(solution)/shard_map/all_to_all | solution.py:120
  106.3 0.9 copy_bitcast_fusion
Async XLA Ops:
  2.1 39.7 %all-to-all-start = ((bf16[32,2,64,128]{3,2,1,0:T(8,128)(2,1)}), bf16[32,2,64,128]{3,2,1,0:T(8,128)(2,1)S(1)}, u32[]{:S(2)}, u32[]{:S(2)}) async-start(bf16[32,2,64,128]{3,2,1,0:T(8,128)(2,1)} %shard_map.55), calls=%async_computation | async-start | bytes 2097152 | tf_op jit(solution)/shard_map/all_to_all | solution.py:120
  41.8 23.8 %collective-permute-start.1 = (bf16[32,2,64,128]{3,2,1,0:T(8,128)(2,1)S(1)}, bf16[32,2,64,128]{3,2,1,0:T(8,128)(2,1)S(1)}, u32[]{:S(2)}, u32[]{:S(2)}) collective-permute-start(bf16[32,2,64,128]{3,2,1,0:T(8,128)(2,1)S(1)} %all-to-all-done.own_hbm), channel_id=1, source_target_pairs={{32,0},{64,32},{96,64},{0,96},{33,1},{65,33},{97,65},{1,97},{34,2}... | collective-permute-start | bytes 3145736 | tf_op jit(solution)/shard_map/ppermute | solution.py:132
  42.3 23.3 %collective-permute-start = (bf16[32,2,64,128]{3,2,1,0:T(8,128)(2,1)S(1)}, bf16[32,2,64,128]{3,2,1,0:T(8,128)(2,1)}, u32[]{:S(2)}, u32[]{:S(2)}) collective-permute-start(bf16[32,2,64,128]{3,2,1,0:T(8,128)(2,1)S(1)} %all-to-all-done.own_hbm), channel_id=1, source_target_pairs={{0,32},{32,64},{64,96},{96,0},{1,33},{33,65},{65,97},{97,1},{2,34}... | collective-permute-start | bytes 3145736 | tf_op jit(solution)/shard_map/ppermute | solution.py:131
  43.8 21.8 %all-to-all-start.1 = ((bf16[32,64,128]{2,1,0:T(8,128)(2,1)}), bf16[32,64,128]{2,1,0:T(8,128)(2,1)S(1)}, u32[]{:S(2)}, u32[]{:S(2)}) async-start(bf16[32,64,128]{2,1,0:T(8,128)(2,1)} %shard_map.56), calls=%async_computation.1 | async-start | bytes 1048576 | tf_op jit(solution)/shard_map/all_to_all | solution.py:120
  49.0 16.6 %copy-start = (s32[16,12]{1,0:T(8,128)S(1)}, s32[16,12]{1,0:T(8,128)}, u32[]{:S(2)}) copy-start(s32[16,12]{1,0:T(8,128)} %tl.1) | copy-start | bytes 2308
  49.1 16.6 %copy-start.1 = (s32[16]{0:T(128)S(1)}, s32[16]{0:T(128)}, u32[]{:S(2)}) copy-start(s32[16]{0:T(128)} %used.1) | copy-start | bytes 196

commit v3 on v2

v3 whole, which is shorter than its diff:
```python
import math

import jax
import jax.numpy as jnp
from jax import lax
from jax.experimental import pallas as pl
from jax.experimental.pallas import tpu as pltpu
from jax.sharding import PartitionSpec as P

HD = 128
TILE = 512
TILES_HERE = 4
SPAN = 12
STEP = 4
SLOTS = 36
LOG2_SCALE = HD ** -0.5 * math.log2(math.e)


def plan_kernel(tile_list, tile_used, blk, key_tile, row_tile, trips):
    first = blk[0] * TILES_HERE
    total = tile_used[first]
    for i in range(1, TILES_HERE):
        total = total + tile_used[first + i]
    split = total > SLOTS

    def add(i, group, filled):
        def put(s, filled):
            key_tile[group, filled] = tile_list[first + i, s] - first + TILES_HERE
            row_tile[group, filled] = jnp.int32(i)
            return filled + 1

        return lax.fori_loop(0, tile_used[first + i], put, filled)

    def close(group, filled):
        for j in range(STEP - 1):
            key_tile[group, filled + j] = jnp.int32(TILES_HERE)
            row_tile[group, filled + j] = jnp.int32(TILES_HERE)
        trips[group] = (filled + (STEP - 1)) // STEP

    filled = jnp.int32(0)
    for i in range(TILES_HERE - 1):
        filled = add(i, 0, filled)
    last_group = split.astype(jnp.int32)
    start = jnp.where(split, 0, filled)
    close(0, filled)
    trips[1] = jnp.int32(0)
    ended = add(TILES_HERE - 1, last_group, start)
    close(last_group, ended)
    trips[2] = last_group + 1


def plan(tile_list, tile_used, blk):
    smem = pl.BlockSpec(memory_space=pltpu.SMEM)
    width = SLOTS + STEP
    return pl.pallas_call(
        plan_kernel,
        in_specs=[smem] * 3,
        out_specs=[smem] * 3,
        out_shape=[
            jax.ShapeDtypeStruct((2, width), jnp.int32),
            jax.ShapeDtypeStruct((2, width), jnp.int32),
            jax.ShapeDtypeStruct((3,), jnp.int32),
        ],
    )(tile_list, tile_used, blk)


def attention_kernel(
    key_tile, row_tile, trips, q_in, low_in, own_in, high_in, out, q_all, kv, scores, tops, sums, sems
):
    near = (own_in, low_in, high_in)
    place = (1, 0, 2)
    third = kv.shape[1] // 3
    first_copies = [pltpu.make_async_copy(q_in, q_all, sems.at[0])]
    later_copies = []
    for j in range(3):
        span = pl.ds(third * place[j], third)
        first_copies.append(pltpu.make_async_copy(near[j].at[:, 0], kv.at[0, span], sems.at[1 + j]))
        later_copies.append(pltpu.make_async_copy(near[j].at[:, 1], kv.at[1, span], sems.at[4 + j]))
    for c in first_copies + later_copies:
        c.start()
    tops[...] = jnp.full(tops.shape, -3e38, jnp.float32)
    sums[...] = jnp.zeros_like(sums)
    for c in first_copies:
        c.wait()

    def group(g, _):
        def score(step, _):
            for j in range(STEP):
                s = step * STEP + j
                row = row_tile[g, s]
                q = q_all[pl.ds(8 * jnp.minimum(row, TILES_HERE - 1), 8)].reshape(TILE, HD)
                k = kv[0, pl.ds(8 * key_tile[g, s], 8)].reshape(TILE, HD)
                dots = lax.dot_general(
                    q, k, (((1,), (1,)), ((), ())), preferred_element_type=jnp.float32
                )
                scores[s] = dots
                lanes = [dots[:, HD * n : HD * (n + 1)] for n in range(TILE // HD)]
                top = jnp.maximum(jnp.maximum(lanes[0], lanes[1]), jnp.maximum(lanes[2], lanes[3]))
                tops[row] = jnp.maximum(tops[row], top)
            return 0

        lax.fori_loop(0, trips[g], score, 0)

        @pl.when(g == 0)
        def _():
            for c in later_copies:
                c.wait()

        for i in range(TILES_HERE):
            top = jnp.max(tops[i], axis=1, keepdims=True) * LOG2_SCALE
            tops[i] = jnp.broadcast_to(top, (TILE, HD))

        def weigh(step, _):
            for j in range(STEP):
                s = step * STEP + j
                row = row_tile[g, s]
                v = kv[1, pl.ds(8 * key_tile[g, s], 8)].reshape(TILE, HD)
                v = jnp.concatenate([v, jnp.ones_like(v)], axis=1)
                top = tops[row]
                weights = [
                    jnp.exp2(scores[s, :, HD * n : HD * (n + 1)] * LOG2_SCALE - top)
                    for n in range(TILE // HD)
                ]
                weights = jnp.concatenate([w.astype(jnp.bfloat16) for w in weights], axis=1)
                sums[row] += jnp.dot(weights, v, preferred_element_type=jnp.float32)
            return 0

        lax.fori_loop(0, trips[g], weigh, 0)
        return 0

    lax.fori_loop(0, trips[2], group, 0)
    for i in range(TILES_HERE):
        result = sums[i, :, :HD] / sums[i, :, HD:]
        out[pl.ds(8 * i, 8)] = result.astype(jnp.bfloat16).reshape(8, TILE // 8, HD)


def attend(planned, q, low, own, high):
    anywhere = pl.BlockSpec(memory_space=pl.ANY)
    return pl.pallas_call(
        attention_kernel,
        grid_spec=pltpu.PrefetchScalarGridSpec(
            num_scalar_prefetch=3,
            grid=(1,),
            in_specs=[anywhere] * 4,
            out_specs=pl.BlockSpec(q.shape, lambda i, *_: (0, 0, 0)),
            scratch_shapes=[
                pltpu.VMEM(q.shape, q.dtype),
                pltpu.VMEM((2, 3 * q.shape[0]) + q.shape[1:], q.dtype),
                pltpu.VMEM((SLOTS, TILE, TILE), jnp.float32),
                pltpu.VMEM((TILES_HERE + 1, TILE, HD), jnp.float32),
                pltpu.VMEM((TILES_HERE + 1, TILE, 2 * HD), jnp.float32),
                pltpu.SemaphoreType.DMA((7,)),
            ],
        ),
        out_shape=jax.ShapeDtypeStruct(q.shape, q.dtype),
        compiler_params=pltpu.CompilerParams(vmem_limit_bytes=49 * 2**20),
        cost_estimate=pl.CostEstimate(
            flops=32 * 4 * TILE * TILE * HD, bytes_accessed=4 * 2**20, transcendentals=32 * TILE * TILE
        ),
    )(*planned, q, low, own, high)


def pack_kernel(*refs):
    ins, out = refs[:-1], refs[-1]
    for h in range(out.shape[0]):
        for a, r in enumerate(ins):
            piece = r[:, HD * h : HD * (h + 1)]
            if len(ins) > 1:
                out[h, a] = piece
            else:
                out[h] = piece


def pack(*arrays):
    rows, width = arrays[0].shape
    heads = width // HD
    steps = 2
    inner = (len(arrays), rows, HD) if len(arrays) > 1 else (rows, HD)
    nbytes = 2 * len(arrays) * rows * width * 2
    return pl.pallas_call(
        pack_kernel,
        grid=(steps,),
        in_specs=[pl.BlockSpec((rows, width // steps), lambda i: (0, i))] * len(arrays),
        out_specs=pl.BlockSpec((heads // steps,) + inner, lambda i: (i,) + (0,) * len(inner)),
        out_shape=jax.ShapeDtypeStruct((heads,) + inner, arrays[0].dtype),
        cost_estimate=pl.CostEstimate(flops=0, bytes_accessed=nbytes, transcendentals=0),
    )(*arrays)


def exchange(x):
    return lax.all_to_all(x, "uly", split_axis=0, concat_axis=0, tiled=True)


def body(queries, key_states, value_states, tile_list, tile_used):
    blk = lax.axis_index("blk").astype(jnp.int32).reshape(1)
    count = lax.axis_size("blk")
    up = [(i, (i + 1) % count) for i in range(count)]
    down = [((i + 1) % count, i) for i in range(count)]
    kv = exchange(pack(key_states, value_states))
    q = pack(queries)
    planned = plan(tile_list, tile_used, blk)
    kv, q, planned = lax.optimization_barrier((kv, q, planned))
    low = lax.ppermute(kv, "blk", up)
    high = lax.ppermute(kv, "blk", down)
    q = exchange(q)
    out = attend(planned, q, low, kv, high)
    out = exchange(out)
    return jnp.transpose(out, (1, 0, 2)).reshape(queries.shape)


def solution(mesh):
    spec = P(("cfg", "blk", "uly"), None)
    return jax.shard_map(
        body,
        mesh=mesh,
        in_specs=(spec, spec, spec, P(), P()),
        out_specs=spec,
        check_vma=False,
    )
```

time: 107 us -> 104 us (0.972); the launches traced: 107 us -> 103 us
  blocking collectives: 22.6 us -> 44.3 us
  waiting for transfers between devices: 43.3 us -> 25.1 us
  starting transfers between devices: 18.4 us -> 13.2 us
  Pallas kernels: 21.9 us -> 19.5 us
    all_to_all x1 -> x2, blocking collectives: 22.6 us -> 44.3 us  [exchange(): return lax.all_to_all(x, 'uly', split_axis=0, concat_axis=0, tiled=True)]
    all_to_all x2 -> x1, waiting for transfers between devices: 43.3 us -> 25 us  [exchange(): return lax.all_to_all(x, 'uly', split_axis=0, concat_axis=0, tiled=True)]
    all_to_all x2 -> x1, starting transfers between devices: 16.4 us -> 11.2 us  [exchange(): return lax.all_to_all(x, 'uly', split_axis=0, concat_axis=0, tiled=True)]
    pallas_call x1 -> x2, Pallas kernels: 18 us -> 15.6 us  [the longest x1 14 us: attend(): pl.pallas_call(attention_kernel, grid_spec=pltpu.PrefetchScalarGridSpec(n...]
  transfers between devices with their start and end apart: 4 -> 3, of which waited for: 2 -> 1; matrix products, arithmetic and copies ran while one was open for 0% -> 0% of each run, Pallas kernels for 2% -> 3%
where the time goes in v3:
time: 104 us; the launch traced here: 103 us
  blocking collectives  44.3 us (43%)
  waiting for transfers between devices  25.1 us (24%)
  Pallas kernels  19.5 us (19%)
  starting transfers between devices  13.2 us (13%)
    all_to_all x2, blocking collectives, exchange(): return lax.all_to_all(x, 'uly', split_axis=0, concat_axis=0, tiled=True)  44.3 us
    all_to_all x1, waiting for transfers between devices, exchange(): return lax.all_to_all(x, 'uly', split_axis=0, concat_axis=0, tiled=True)  25 us
    pallas_call x1, Pallas kernels, attend(): pl.pallas_call(attention_kernel, grid_spec=pltpu.PrefetchScalarGridSpec(n...  14 us
    all_to_all x1, starting transfers between devices, exchange(): return lax.all_to_all(x, 'uly', split_axis=0, concat_axis=0, tiled=True)  11.2 us
    pallas_call x2, Pallas kernels, pack(): pl.pallas_call(pack_kernel, grid=(steps,), in_specs=[pl.BlockSpec((rows,...  3.89 us
  transfers between devices with their start and end apart: 3, of which 1 were waited for; matrix products, arithmetic and copies ran while one was open for 0% of the time, Pallas kernels for 3%

profile of v3, /device:TPU:48, one launch (start us, length us, event | category | flops | bytes accessed | tf_op | source)
XLA Modules:
  0.0 103.0 jit_solution(17699252545486524338)
XLA Ops:
  0.0 2.1 %shard_map.55 = bf16[32,2,64,128]{3,2,1,0:T(8,128)(2,1)} custom-call(bf16[64,4096]{1,0:T(8,128)(2,1)} %refs_0_.2, bf16[64,4096]{1,0:T(8,128)(2,1)} %refs_1_.1), custom_call_target="tpu_custom_call" | custom-call | bytes 2097152 | tf_op jit(solution)/shard_map/pallas_call | solution.py:180
  2.1 11.2 %all-to-all-start = ((bf16[32,2,64,128]{3,2,1,0:T(8,128)(2,1)}), bf16[32,2,64,128]{3,2,1,0:T(8,128)(2,1)S(1)}, u32[]{:S(2)}, u32[]{:S(2)}) async-start(bf16[32,2,64,128]{3,2,1,0:T(8,128)(2,1)} %shard_map.55), calls=%async_computation | async-start | bytes 2097152 | tf_op jit(solution)/shard_map/all_to_all | solution.py:191
  13.3 1.8 %shard_map.56 = bf16[32,64,128]{2,1,0:T(8,128)(2,1)} custom-call(bf16[64,4096]{1,0:T(8,128)(2,1)} %refs_0_.3), custom_call_target="tpu_custom_call" | custom-call | bytes 1048576 | tf_op jit(solution)/shard_map/pallas_call | solution.py:180
  15.1 1.7 %shard_map.57 = (s32[2,40]{1,0:T(2,128)}, s32[2,40]{1,0:T(2,128)}, s32[3]{0:T(128)}) custom-call(s32[16,12]{1,0:T(8,128)} %tile_list.1, s32[16]{0:T(128)} %tile_used.1, s32[1]{0:T(128)} %bitcast.blk), custom_call_target="tpu_custom_call" | custom-call | tf_op jit(solution)/shard_map/pallas_call | solution.py:55
  16.8 25.0 %all-to-all-done.own_in = bf16[32,2,64,128]{3,2,1,0:T(8,128)(2,1)S(1)} async-done(((bf16[32,2,64,128]{3,2,1,0:T(8,128)(2,1)}), bf16[32,2,64,128]{3,2,1,0:T(8,128)(2,1)S(1)}, u32[]{:S(2)}, u32[]{:S(2)}) %all-to-all-start) | async-done | bytes 1048608 | tf_op jit(solution)/shard_map/all_to_all | solution.py:191
  41.8 0.0 copy-start
  41.8 0.0 copy-start.1
  41.8 0.0 copy-start.2
  41.8 0.4 collective-permute-start.1
  42.3 1.6 %collective-permute-start = (bf16[32,2,64,128]{3,2,1,0:T(8,128)(2,1)S(1)}, bf16[32,2,64,128]{3,2,1,0:T(8,128)(2,1)S(1)}, u32[]{:S(2)}, u32[]{:S(2)}) collective-permute-start(bf16[32,2,64,128]{3,2,1,0:T(8,128)(2,1)S(1)} %all-to-all-done.own_in), channel_id=1, source_target_pairs={{0,32},{32,64},{64,96},{96,0},{1,33},{33,65},{65,97},{97,1},{2,34}... | collective-permute-start | bytes 3145736 | tf_op jit(solution)/shard_map/ppermute | solution.py:203
  43.8 21.8 %all_to_all.15.q_in = bf16[32,64,128]{2,1,0:T(8,128)(2,1)S(1)} all-to-all(bf16[32,64,128]{2,1,0:T(8,128)(2,1)} %shard_map.56), channel_id=1, replica_groups=mesh['cfg'=2,'blk'=4,'uly'=32] {'uly'}, dimensions={0} | all-to-all | bytes 1048576 | tf_op jit(solution)/shard_map/all_to_all | solution.py:191
  65.6 0.0 collective-permute-done.1.high_in
  65.6 0.0 collective-permute-done.low_in
  65.6 0.0 copy-done
  65.6 0.0 copy-done.1
  65.6 0.0 copy-done.2
  65.6 14.0 %shard_map.58 = bf16[32,64,128]{2,1,0:T(8,128)(2,1)S(1)} custom-call(s32[2,40]{1,0:T(2,128)S(1)} %copy-done, s32[2,40]{1,0:T(2,128)S(1)} %copy-done.1, s32[3]{0:T(128)S(1)} %copy-done.2, bf16[32,64,128]{2,1,0:T(8,128)(2,1)S(1)} %all_to_all.15.q_in, bf16[32,2,64,128]{3,2,1,0:T(8,128)(2,1)S(1)} %collective-permute-done.low_in, ...), custom_call_target="tpu_custom_call" | custom-call | flops 4294967296 | bytes 4194304 | tf_op jit(solution)/shard_map/pallas_call | solution.py:139
  79.6 22.5 %all_to_all.16 = bf16[32,64,128]{2,1,0:T(8,128)(2,1)S(1)} all-to-all(bf16[32,64,128]{2,1,0:T(8,128)(2,1)S(1)} %shard_map.58), channel_id=1, replica_groups=mesh['cfg'=2,'blk'=4,'uly'=32] {'uly'}, dimensions={0} | all-to-all | bytes 1048576 | tf_op jit(solution)/shard_map/all_to_all | solution.py:191
  102.1 0.9 copy_bitcast_fusion
Async XLA Ops:
  2.1 39.7 %all-to-all-start = ((bf16[32,2,64,128]{3,2,1,0:T(8,128)(2,1)}), bf16[32,2,64,128]{3,2,1,0:T(8,128)(2,1)S(1)}, u32[]{:S(2)}, u32[]{:S(2)}) async-start(bf16[32,2,64,128]{3,2,1,0:T(8,128)(2,1)} %shard_map.55), calls=%async_computation | async-start | bytes 2097152 | tf_op jit(solution)/shard_map/all_to_all | solution.py:191
  41.8 23.8 %copy-start = (s32[2,40]{1,0:T(2,128)S(1)}, s32[2,40]{1,0:T(2,128)}, u32[]{:S(2)}) copy-start(s32[2,40]{1,0:T(2,128)} %get-tuple-element.16.key_tile) | copy-start | bytes 964
  41.8 23.8 %copy-start.1 = (s32[2,40]{1,0:T(2,128)S(1)}, s32[2,40]{1,0:T(2,128)}, u32[]{:S(2)}) copy-start(s32[2,40]{1,0:T(2,128)} %get-tuple-element.17.row_tile) | copy-start | bytes 964
  41.8 23.8 %copy-start.2 = (s32[3]{0:T(128)S(1)}, s32[3]{0:T(128)}, u32[]{:S(2)}) copy-start(s32[3]{0:T(128)} %get-tuple-element.18.trips) | copy-start | bytes 40
  41.8 23.8 %collective-permute-start.1 = (bf16[32,2,64,128]{3,2,1,0:T(8,128)(2,1)S(1)}, bf16[32,2,64,128]{3,2,1,0:T(8,128)(2,1)S(1)}, u32[]{:S(2)}, u32[]{:S(2)}) collective-permute-start(bf16[32,2,64,128]{3,2,1,0:T(8,128)(2,1)S(1)} %all-to-all-done.own_in), channel_id=1, source_target_pairs={{32,0},{64,32},{96,64},{0,96},{33,1},{65,33},{97,65},{1,97},{34,2}... | collective-permute-start | bytes 3145736 | tf_op jit(solution)/shard_map/ppermute | solution.py:204
  42.3 23.3 %collective-permute-start = (bf16[32,2,64,128]{3,2,1,0:T(8,128)(2,1)S(1)}, bf16[32,2,64,128]{3,2,1,0:T(8,128)(2,1)S(1)}, u32[]{:S(2)}, u32[]{:S(2)}) collective-permute-start(bf16[32,2,64,128]{3,2,1,0:T(8,128)(2,1)S(1)} %all-to-all-done.own_in), channel_id=1, source_target_pairs={{0,32},{32,64},{64,96},{96,0},{1,33},{33,65},{65,97},{97,1},{2,34}... | collective-permute-start | bytes 3145736 | tf_op jit(solution)/shard_map/ppermute | solution.py:203
